TPU v7x, 32 devices: a whole 2x2x4 slice. The times are simulated.
32 devices in a mesh: ep: 16 (over z, y, core), dp: 2 (over x).
Axes of the slice: x: 2, y: 2, z: 4, core: 2. Of those that a mesh axis runs over, the one named last changes fastest.
Arguments:
- hidden: bfloat16 [2, 1024, 2048], P(None, ('ep', 'dp')), may hold values from -6 to 6
- norm_gain: bfloat16 [2048], replicated, may hold values from 0.5 to 1.5
- gate_weights: float32 [2, 1024, 8], P(None, ('ep', 'dp')), may hold values from 0.05 to 1
- routes: int32 [2, 1024, 8], P(None, ('ep', 'dp')), may hold values from 0 to 15, as said below
- replica_pick: int32 [2, 1024, 8], P(None, ('ep', 'dp')), may hold values from 0 to 1023
- trainer_experts: int32 [16], replicated, may hold values from 0 to 15, each once
- hot_experts: int32 [3], replicated, may hold values from 0 to 15, as said below
- replica_hot: int32 [16], replicated, may hold values from 0 to 2, as said below
- w_gate: bfloat16 [16, 2048, 384], P('ep', 'dp'), may hold values from -0.125 to 0.125
- w_up: bfloat16 [16, 2048, 384], P('ep', 'dp'), may hold values from -0.125 to 0.125
- w_down: bfloat16 [16, 384, 2048], P('ep', None, 'dp'), may hold values from -0.3125 to 0.3125
- queries: bfloat16 [2, 1024, 4096], P(None, ('ep', 'dp')), may hold values from -6 to 6
- key_cache: bfloat16 [1024, 32, 512], P(('ep', 'dp')), may hold values from -6 to 6
- value_cache: bfloat16 [1024, 32, 512], P(('ep', 'dp')), may hold values from -6 to 6
- new_keys: bfloat16 [2, 1024, 512], P(None, ('ep', 'dp')), may hold values from -6 to 6
- new_values: bfloat16 [2, 1024, 512], P(None, ('ep', 'dp')), may hold values from -6 to 6
- cache_lengths: int32 [1024], P(('ep', 'dp')), may hold values from 2 to 32, as said below
Outputs:
- mixed: bfloat16 [2, 1024, 2048], P(None, ('ep', 'dp'))
- context: bfloat16 [2, 1024, 4096], P(None, ('ep', 'dp'))
Inputs may be any that keep to these rules, and one draw needn't show every extreme that they name: Trainer index p holds expert trainer_experts[p]; each expert once. `hot_experts`: 3 different experts, among them expert 0 and expert 16 - 1. `replica_hot`: every entry of hot_experts is named by some index. `cache_lengths`: the 32 sequences of each device include one with 32 live entries. `routes`: each row names 8 different experts; every expert is named by some row.
All inputs are finite; a program needn't handle non-finite values.
Results may differ from a plain program's by a relative error of at most 0.001.
The roundings to bfloat16 on the way count: a program that leaves them out, or rounds other values in their place, can miss the bound.
Values may be sent and summed in bfloat16 or wider, within the bound.
No kernel may reach another device: no remote copies, remote signals or barrier semaphores. Data moves between devices by JAX's collectives and lax.ppermute only.
A program may use at most 64 MiB of HBM per device.

v0:
```python
import math
import jax
import jax.numpy as jnp
from jax import lax
from jax.sharding import PartitionSpec as P

HEADS = 32
KV_HEADS = 4
HEAD = 128
TOP = 8
CAP = 3
SLOTS = 2
norm_epsilon = 1e-06


def spread(shard, axis, root):
    mine = lax.axis_index(axis) == root
    return lax.psum(jnp.where(mine, shard, jnp.zeros_like(shard)), axis)


def scaled_norm(hidden_rows, norm_gain):
    values = hidden_rows.astype(jnp.float32)
    mean_square = jnp.mean(values * values, axis=-1, keepdims=True)
    return (values * lax.rsqrt(mean_square + norm_epsilon) * norm_gain.astype(jnp.float32)).astype(
        jnp.bfloat16
    )


def table_lookup(onehot_rows, table):
    return jnp.dot(onehot_rows, table, preferred_element_type=jnp.int32)


def attend(query_rows, key_cache, value_cache, new_keys, new_values, cache_lengths, step_index):
    rows_here = query_rows.shape[0]
    cache_len = key_cache.shape[1]
    steps_all = new_keys.shape[0]
    grouped = query_rows.reshape(rows_here, KV_HEADS, HEADS // KV_HEADS, HEAD)
    keys_cached = key_cache.reshape(rows_here, cache_len, KV_HEADS, HEAD)
    values_cached = value_cache.reshape(rows_here, cache_len, KV_HEADS, HEAD)
    keys_fresh = new_keys.reshape(steps_all, rows_here, KV_HEADS, HEAD)
    values_fresh = new_values.reshape(steps_all, rows_here, KV_HEADS, HEAD)
    score_scale = 1.0 / math.sqrt(HEAD)
    cache_scores = (
        jnp.einsum("rkgh,rckh->rkgc", grouped, keys_cached, preferred_element_type=jnp.float32)
        * score_scale
    )
    fresh_scores = (
        jnp.einsum("rkgh,srkh->rkgs", grouped, keys_fresh, preferred_element_type=jnp.float32)
        * score_scale
    )
    cache_mask = (jnp.arange(cache_len, dtype=jnp.int32)[None, :] < cache_lengths[:, None])[
        :, None, None, :
    ]
    fresh_mask = (jnp.arange(steps_all, dtype=jnp.int32) <= step_index)[None, None, None, :]
    row_max = jnp.maximum(
        jnp.max(jnp.where(cache_mask, cache_scores, -1e30), axis=-1),
        jnp.max(jnp.where(fresh_mask, fresh_scores, -1e30), axis=-1),
    )
    cache_exp = jnp.where(cache_mask, jnp.exp(cache_scores - row_max[..., None]), 0.0)
    fresh_exp = jnp.where(fresh_mask, jnp.exp(fresh_scores - row_max[..., None]), 0.0)
    row_total = jnp.sum(cache_exp, axis=-1) + jnp.sum(fresh_exp, axis=-1)
    cache_probs = (cache_exp / row_total[..., None]).astype(jnp.bfloat16)
    fresh_probs = (fresh_exp / row_total[..., None]).astype(jnp.bfloat16)
    summed = jnp.einsum(
        "rkgc,rckh->rkgh", cache_probs, values_cached, preferred_element_type=jnp.float32
    )
    summed = summed + jnp.einsum(
        "rkgs,srkh->rkgh", fresh_probs, values_fresh, preferred_element_type=jnp.float32
    )
    return summed.astype(jnp.bfloat16).reshape(rows_here, HEADS * HEAD)


def body(
    hidden,
    norm_gain,
    gate_weights,
    routes,
    replica_pick,
    trainer_experts,
    hot_experts,
    replica_hot,
    w_gate,
    w_up,
    w_down,
    queries,
    key_cache,
    value_cache,
    new_keys,
    new_values,
    cache_lengths,
):
    ep_count = lax.axis_size("ep")
    my_device = lax.axis_index("ep")
    device_ids = jnp.arange(ep_count, dtype=jnp.int32)
    expert_count = trainer_experts.shape[0]
    expert_ids = jnp.arange(expert_count, dtype=jnp.int32)
    hot_count = hot_experts.shape[0]
    hot_ids = jnp.arange(hot_count, dtype=jnp.int32)
    home_device = jnp.sum(
        jnp.where(trainer_experts[None, :] == expert_ids[:, None], device_ids[None, :], 0), axis=1
    )
    hosted = jnp.sum(
        jnp.where(replica_hot[:, None] == hot_ids[None, :], hot_experts[None, :], 0), axis=1
    )
    is_replica = (hosted[None, :] == expert_ids[:, None]).astype(jnp.int32)
    replica_order = jnp.cumsum(is_replica, axis=1) * is_replica
    copies = 1 + jnp.sum(is_replica, axis=1)
    my_hot = jnp.sum(jnp.where(device_ids == my_device, replica_hot, 0))
    own_pair = jnp.concatenate([w_gate, w_up], axis=0)
    own_full_pair, own_full_down = (
        lax.all_gather(own_pair, "dp", axis=1, tiled=True),
        lax.all_gather(w_down, "dp", axis=2, tiled=True),
    )
    replica_pair = jnp.zeros_like(own_pair)
    replica_down = jnp.zeros_like(w_down)
    for hot_index in range(hot_count):
        hot_expert = jnp.sum(jnp.where(hot_ids == hot_index, hot_experts, 0))
        root_device = jnp.sum(jnp.where(expert_ids == hot_expert, home_device, 0))
        sent_pair, sent_down = (
            spread(own_pair, "ep", root_device),
            spread(w_down, "ep", root_device),
        )
        wanted = my_hot == hot_index
        replica_pair = jnp.where(wanted, sent_pair, replica_pair)
        replica_down = jnp.where(wanted, sent_down, replica_down)
    replica_full_pair, replica_full_down = (
        lax.all_gather(replica_pair, "dp", axis=1, tiled=True),
        lax.all_gather(replica_down, "dp", axis=2, tiled=True),
    )
    slot_pair = jnp.stack([own_full_pair, replica_full_pair])
    slot_down = jnp.concatenate([own_full_down, replica_full_down], axis=0)
    tokens_here = hidden.shape[1]
    width = hidden.shape[2]
    entries = tokens_here * TOP
    slot_total = ep_count * SLOTS
    buffer_rows = slot_total * CAP
    entry_ids = jnp.arange(entries, dtype=jnp.int32)
    token_map = (
        (entry_ids // TOP)[:, None] == jnp.arange(tokens_here, dtype=jnp.int32)[None, :]
    ).astype(jnp.float32)
    contract_first = (((0,), (0,)), ((), ()))
    mixed_steps = []
    context_steps = []
    for step_index in range(hidden.shape[0]):
        context_steps.append(
            attend(
                queries[step_index],
                key_cache,
                value_cache,
                new_keys,
                new_values,
                cache_lengths,
                step_index,
            )
        )
        normed = scaled_norm(hidden[step_index], norm_gain)
        weights_top = gate_weights[step_index]
        gates = (weights_top / jnp.sum(weights_top, axis=-1, keepdims=True)).astype(jnp.bfloat16)
        chosen = routes[step_index].reshape(entries)
        replica_picks = replica_pick[step_index].reshape(entries)
        expert_onehot = (chosen[:, None] == expert_ids[None, :]).astype(jnp.int32)
        replica_index = replica_picks % table_lookup(expert_onehot, copies)
        order_rows = table_lookup(expert_onehot, replica_order)
        replica_device = jnp.sum(
            jnp.where(order_rows == replica_index[:, None], device_ids[None, :], 0), axis=1
        )
        target = jnp.where(
            replica_index == 0, table_lookup(expert_onehot, home_device), replica_device
        )
        second_slot = (replica_index > 0).astype(jnp.int32)
        slot_index = target * SLOTS + second_slot
        slot_onehot = (
            slot_index[:, None] == jnp.arange(slot_total, dtype=jnp.int32)[None, :]
        ).astype(jnp.int32)
        slot_rank = jnp.sum(jnp.cumsum(slot_onehot, axis=0) * slot_onehot, axis=1) - 1
        is_kept = slot_rank < CAP
        row_index = second_slot * (ep_count * CAP) + target * CAP + slot_rank
        placed = (
            is_kept[:, None]
            & (row_index[:, None] == jnp.arange(buffer_rows, dtype=jnp.int32)[None, :])
        ).astype(jnp.float32)
        dispatch = lax.dot_general(placed, token_map, contract_first).astype(jnp.bfloat16)
        weighted = placed * gates.reshape(entries).astype(jnp.float32)[:, None]
        combine_map = lax.dot_general(token_map, weighted, contract_first).astype(jnp.bfloat16)
        outgoing = jnp.dot(dispatch, normed, preferred_element_type=jnp.float32).astype(
            jnp.bfloat16
        )
        outgoing = outgoing.reshape(SLOTS, ep_count, CAP, width)
        incoming = lax.all_to_all(outgoing, "ep", split_axis=1, concat_axis=1, tiled=True)
        slot_rows = incoming.reshape(SLOTS, ep_count * CAP, width)
        projected = jnp.einsum(
            "snd,skdf->sknf", slot_rows, slot_pair, preferred_element_type=jnp.float32
        )
        hidden_units = (jax.nn.silu(projected[:, 0]) * projected[:, 1]).astype(jnp.bfloat16)
        expert_out = jnp.einsum(
            "snf,sfd->snd", hidden_units, slot_down, preferred_element_type=jnp.float32
        ).astype(jnp.bfloat16)
        expert_out = expert_out.reshape(SLOTS, ep_count, CAP, width)
        returned = lax.all_to_all(
            expert_out, "ep", split_axis=1, concat_axis=1, tiled=True
        ).reshape(buffer_rows, width)
        mixed_rows = hidden[step_index].astype(jnp.float32) + jnp.dot(
            combine_map, returned, preferred_element_type=jnp.float32
        )
        mixed_steps.append(mixed_rows.astype(jnp.bfloat16))
    return (jnp.stack(mixed_steps), jnp.stack(context_steps))


def solution(mesh):
    return jax.shard_map(
        body,
        mesh=mesh,
        in_specs=(
            P(None, ("ep", "dp"), None),
            P(),
            P(None, ("ep", "dp"), None),
            P(None, ("ep", "dp"), None),
            P(None, ("ep", "dp"), None),
            P(),
            P(),
            P(),
            P("ep", "dp", None),
            P("ep", "dp", None),
            P("ep", None, "dp"),
            P(None, ("ep", "dp"), None),
            P(("ep", "dp"), None, None),
            P(("ep", "dp"), None, None),
            P(None, ("ep", "dp"), None),
            P(None, ("ep", "dp"), None),
            P(("ep", "dp")),
        ),
        out_specs=(P(None, ("ep", "dp"), None), P(None, ("ep", "dp"), None)),
        check_vma=False,
    )
```

profile of v0, /device:TPU:0, one launch (start us, length us, event | category | flops | bytes accessed | tf_op | source)
XLA Modules:
  0.0 346.7 jit_solution(13511546393007678465)
XLA Ops:
  8.1 1.5 fusion.144
  9.5 0.8 select_reduce_fusion.4
  10.3 2.7 fusion.145
  14.9 1.2 constant_dynamic-update-slice_fusion.1
  16.1 1.3 constant_dynamic-update-slice_fusion
  17.4 2.3 broadcast_select_fusion
  19.7 0.3 copy-done.3
  20.1 1.5 broadcast_select_fusion.3
  21.6 0.5 all-gather.9.cloned.1.call-update
  22.2 0.6 fusion.139
  25.1 0.6 fusion.171
  26.2 0.2 fusion.61
  26.6 0.3 fusion.13
  26.9 0.2 fusion.60
  27.1 148.3 %all-reduce.3.cloned.1.call-done = (bf16[1,384,1024]{2,1,0:T(8,128)(2,1)}, bf16[1,384,1024]{2,1,0:T(8,128)(2,1)}, bf16[1,384,1024]{2,1,0:T(8,128)(2,1)}, bf16[2,...) async-done(((bf16[1,384,1024]{2,1,0:T(8,128)(2,1)}, bf16[1,384,1024]{2,1,0:T(8,128)(2,1)}, bf16[1,384,1024]{2,1,0:T(8,128)(2,1)}, ...) | async-done | bytes 7077904 | tf_op jit(solution)/shard_map/psum | solution.py:18
  175.4 2.1 select_select_fusion.1
  177.6 0.6 reduce-window.14
  178.7 0.5 add_rsqrt_fusion
  179.3 0.6 copy-done.12
  179.8 0.6 convolution_convert_fusion.3
  180.5 0.2 reshape.204
  180.8 1.2 copy.85
  182.0 5.0 %all-to-all-start = ((bf16[2,16,3,2048]{3,0,2,1:T(2,128)(2,1)}), bf16[2,16,3,2048]{3,0,2,1:T(2,128)(2,1)S(1)}, u32[]{:S(2)}, u32[]{:S(2)}) async-start(bf16[2,16,3,2048]{3,0,2,1:T(2,128)(2,1)} %copy.85), calls=%async_computation | async-start | bytes 786432 | tf_op jit(solution)/shard_map/all_to_all | solution.py:189
  187.1 0.5 all-gather.5.cloned.1.call-update
  189.0 0.3 fusion.14
  189.6 0.6 reduce-window.16
  190.6 0.6 convolution_convert_fusion.1
  191.2 0.2 reshape.209
  191.4 1.2 copy.94
  192.6 0.7 iota_compare_fusion.23
  193.4 2.9 select_select_fusion
  196.3 0.4 select_reduce_fusion.3
  196.7 0.8 select_reduce_fusion.1
  197.5 1.2 select_reduce_fusion.2
  198.7 0.8 fusion.23
  199.6 0.5 fusion.168
  200.2 0.4 fusion.24
  200.6 0.4 fusion.78
  201.1 0.4 fusion.79
  201.5 0.5 fusion.6
  202.0 0.5 fusion.7
  202.5 2.7 constant_dynamic-update-slice_fusion.3
  205.3 2.8 constant_dynamic-update-slice_fusion.2
  208.1 6.0 %all-to-all-start.2 = ((bf16[2,16,3,2048]{3,0,2,1:T(2,128)(2,1)}), bf16[2,16,3,2048]{3,0,2,1:T(2,128)(2,1)S(1)}, u32[]{:S(2)}, u32[]{:S(2)}) async-start(bf16[2,16,3,2048]{3,0,2,1:T(2,128)(2,1)} %copy.94), calls=%async_computation.2 | async-start | bytes 786432 | tf_op jit(solution)/shard_map/all_to_all | solution.py:189
  214.1 37.0 %all-gather.5.cloned.1.call-done = bf16[2,2048,384]{2,1,0:T(8,128)(2,1)} async-done(((bf16[2,1024,384]{2,1,0:T(8,128)(2,1)}), bf16[2,2048,384]{2,1,0:T(8,128)(2,1)}) %all-gather.5.cloned.1.call-update) | async-done | bytes 3145744 | tf_op jit(solution)/shard_map/all_gather | solution.py:111
  251.1 46.4 %all-gather.7.cloned.1.call-done = bf16[2,2048,384]{2,1,0:T(8,128)(2,1)} async-done(((bf16[2,1024,384]{2,1,0:T(8,128)(2,1)}), bf16[2,2048,384]{2,1,0:T(8,128)(2,1)}) %all-gather.7.cloned.1.call-update) | async-done | bytes 3145744 | tf_op jit(solution)/shard_map/all_gather | solution.py:127
  297.5 3.6 %convolution_bitcast_fusion = f32[2,2,48,384]{3,2,1,0:T(8,128)S(1)} fusion(bf16[2,48,2048,1]{2,0,1,3:T(2,128)(2,1)S(1)} %bitcast.161, bf16[1,2,2048,384]{3,2,1,0:T(8,128)(2,1)} %bitcast.175, bf16[1,2,2048,384]{3,2,1,0:T(8,128)(2,1)} %bitcast.173), kind=kOutput, calls=%fused_computation.24 | convolution fusion | flops 314572800 | bytes 6979584 | tf_op jit(solution)/shard_map/snd,skdf->sknf/dot_general | solution.py:191
  301.2 0.6 convolution_convert_fusion.2
  301.9 1.2 copy.88
  303.0 5.6 %all-to-all-start.1 = ((bf16[2,16,3,2048]{3,0,2,1:T(2,128)(2,1)}), bf16[2,16,3,2048]{3,0,2,1:T(2,128)(2,1)S(1)}, u32[]{:S(2)}, u32[]{:S(2)}) async-start(bf16[2,16,3,2048]{3,0,2,1:T(2,128)(2,1)} %bitcast.15), calls=%async_computation.1 | async-start | bytes 786432 | tf_op jit(solution)/shard_map/all_to_all | solution.py:199
  308.7 3.6 %fusion.8 = f32[2,2,48,384]{3,2,0,1:T(8,128)S(1)} fusion(bf16[2,48,2048]{2,0,1:T(2,128)(2,1)S(1)} %bitcast.162, bf16[1,2,2048,384]{3,2,1,0:T(8,128)(2,1)} %bitcast.176, bf16[1,2,2048,384]{3,2,1,0:T(8,128)(2,1)} %bitcast.174), kind=kOutput, calls=%fused_computation.23 | convolution fusion | flops 305135616 | bytes 6979584 | tf_op jit(solution)/shard_map/snd,skdf->sknf/dot_general | solution.py:191
  312.4 0.7 convolution_convert_fusion
  313.1 1.2 copy.97
  314.2 6.6 %all-to-all-done.1 = bf16[2,16,3,2048]{3,0,2,1:T(2,128)(2,1)S(1)} async-done(((bf16[2,16,3,2048]{3,0,2,1:T(2,128)(2,1)}), bf16[2,16,3,2048]{3,0,2,1:T(2,128)(2,1)S(1)}, u32[]{:S(2)}, u32[]{:S(2)}) %all-to-all-start.1) | async-done | bytes 393248 | tf_op jit(solution)/shard_map/all_to_all | solution.py:199
  320.8 3.7 %all-to-all-start.3 = ((bf16[2,16,3,2048]{3,0,2,1:T(2,128)(2,1)}), bf16[2,16,3,2048]{3,0,2,1:T(2,128)(2,1)S(1)}, u32[]{:S(2)}, u32[]{:S(2)}) async-start(bf16[2,16,3,2048]{3,0,2,1:T(2,128)(2,1)} %bitcast.30), calls=%async_computation.3 | async-start | bytes 786432 | tf_op jit(solution)/shard_map/all_to_all | solution.py:199
  325.1 0.8 pad_maximum_fusion.1
  326.0 0.3 copy.89
  326.3 0.3 reshape.207
  326.6 10.1 %all-to-all-done.3 = bf16[2,16,3,2048]{3,0,2,1:T(2,128)(2,1)S(1)} async-done(((bf16[2,16,3,2048]{3,0,2,1:T(2,128)(2,1)}), bf16[2,16,3,2048]{3,0,2,1:T(2,128)(2,1)S(1)}, u32[]{:S(2)}, u32[]{:S(2)}) %all-to-all-start.3) | async-done | bytes 393248 | tf_op jit(solution)/shard_map/all_to_all | solution.py:199
  336.7 0.3 copy.98
  336.9 0.3 reshape.212
  337.3 0.5 fusion.5
  337.8 0.5 fusion.4
  338.4 0.7 pad_maximum_fusion.2
  (132 shorter events, 4.6 us)
Async XLA Ops:
  8.0 193.5 %copy-start = (bf16[32,32,512]{2,1,0:T(8,128)(2,1)S(1)}, bf16[32,32,512]{2,1,0:T(8,128)(2,1)}, u32[]{:S(2)}) copy-start(bf16[32,32,512]{2,1,0:T(8,128)(2,1)} %param.30) | copy-start | bytes 3145732
  8.0 167.4 %all-reduce.3.cloned.1.call-start = ((), (), s32[]{:S(2)}) async-start(), calls=%async_computation.8 | async-start | bytes 14155776 | tf_op jit(solution)/shard_map/psum | solution.py:18
  10.3 16.5 %copy-start.23 = (s32[16]{0:T(128)}, s32[16]{0:T(128)S(1)}, u32[]{:S(2)}) copy-start(s32[16]{0:T(128)S(1)} %select_reduce_fusion.4) | copy-start | bytes 196
  17.4 2.7 copy-start.3
  17.4 2.7 copy-start.4
  21.5 0.7 copy-start.28
  21.5 1.3 copy-start.27
  21.5 3.4 copy-start.14
  21.5 3.6 %copy-start.15 = (s32[2,32,8]{1,2,0:T(8,128)S(1)}, s32[2,32,8]{1,2,0:T(8,128)}, u32[]{:S(2)}) copy-start(s32[2,32,8]{1,2,0:T(8,128)} %param.21) | copy-start | bytes 6148
  21.6 156.8 %copy-start.19 = (bf16[2048]{0:T(1024)(128)(2,1)S(1)}, bf16[2048]{0:T(1024)(128)(2,1)}, u32[]{:S(2)}) copy-start(bf16[2048]{0:T(1024)(128)(2,1)} %param.18) | copy-start | bytes 12292
  21.6 156.9 %copy-start.5 = (bf16[2,32,2048]{2,1,0:T(8,128)(2,1)S(1)}, bf16[2,32,2048]{2,1,0:T(8,128)(2,1)}, u32[]{:S(2)}) copy-start(bf16[2,32,2048]{2,1,0:T(8,128)(2,1)} %param.17) | copy-start | bytes 786436
  21.6 180.9 %all-gather.9.cloned.1.call-start = ((), (), s32[]{:S(2)}) async-start(), calls=%async_computation.6 | async-start | bytes 2359296 | tf_op jit(solution)/shard_map/all_gather | solution.py:112
  22.2 183.1 %all-gather.11.cloned.1.call-start = ((), (), s32[]{:S(2)}) async-start(), calls=%async_computation.7 | async-start | bytes 2359296 | tf_op jit(solution)/shard_map/all_gather | solution.py:128
  23.0 3.6 %copy-start.25 = (s32[16]{0:T(128)}, s32[16]{0:T(128)S(1)}, u32[]{:S(2)}) copy-start(s32[16]{0:T(128)S(1)} %select_reduce_fusion.5) | copy-start | bytes 196
  26.0 153.2 %copy-start.17 = (s32[16,16]{1,0:T(8,128)}, s32[16,16]{1,0:T(8,128)S(1)}, u32[]{:S(2)}) copy-start(s32[16,16]{1,0:T(8,128)S(1)} %reduce_window_sum.36) | copy-start | bytes 3076
  26.2 153.1 %copy-start.29 = (s32[16]{0:T(128)}, s32[16]{0:T(128)S(1)}, u32[]{:S(2)}) copy-start(s32[16]{0:T(128)S(1)} %fusion.138) | copy-start | bytes 196
  177.5 10.1 %copy-start.7 = (bf16[2,32,4096]{2,1,0:T(8,128)(2,1)S(1)}, bf16[2,32,4096]{2,1,0:T(8,128)(2,1)}, u32[]{:S(2)}) copy-start(bf16[2,32,4096]{2,1,0:T(8,128)(2,1)} %param.28) | copy-start | bytes 1572868
  178.7 0.6 copy-start.20
  179.3 0.6 copy-start.12
  179.8 7.9 %copy-start.8 = (bf16[2,32,512]{2,1,0:T(8,128)(2,1)S(1)}, bf16[2,32,512]{2,1,0:T(8,128)(2,1)}, u32[]{:S(2)}) copy-start(bf16[2,32,512]{2,1,0:T(8,128)(2,1)} %param.31) | copy-start | bytes 196612
  180.4 7.4 %copy-start.9 = (bf16[2,32,512]{2,1,0:T(8,128)(2,1)S(1)}, bf16[2,32,512]{2,1,0:T(8,128)(2,1)}, u32[]{:S(2)}) copy-start(bf16[2,32,512]{2,1,0:T(8,128)(2,1)} %param.32) | copy-start | bytes 196612
  180.7 7.2 %copy-start.16 = (f32[2,32,8]{1,2,0:T(8,128)S(1)}, f32[2,32,8]{1,2,0:T(8,128)}, u32[]{:S(2)}) copy-start(f32[2,32,8]{1,2,0:T(8,128)} %param.19) | copy-start | bytes 6148
  180.7 7.7 %copy-start.11 = (s32[1,32,8]{1,2,0:T(8,128)S(1)}, s32[1,32,8]{1,2,0:T(8,128)}, u32[]{:S(2)}) copy-start(s32[1,32,8]{1,2,0:T(8,128)} %get-tuple-element.32) | copy-start | bytes 3076
  180.7 7.9 %copy-start.30 = (s32[16]{0:T(128)S(1)}, s32[16]{0:T(128)}, u32[]{:S(2)}) copy-start(s32[16]{0:T(128)} %copy-done.29) | copy-start | bytes 196
  180.7 8.3 %copy-start.18 = (s32[16,16]{1,0:T(8,128)S(1)}, s32[16,16]{1,0:T(8,128)}, u32[]{:S(2)}) copy-start(s32[16,16]{1,0:T(8,128)} %copy-done.17) | copy-start | bytes 3076
  180.7 8.3 %copy-start.26 = (s32[16]{0:T(128)S(1)}, s32[16]{0:T(128)}, u32[]{:S(2)}) copy-start(s32[16]{0:T(128)} %copy-done.25) | copy-start | bytes 196
  180.7 8.6 %copy-start.24 = (s32[16]{0:T(128)S(1)}, s32[16]{0:T(128)}, u32[]{:S(2)}) copy-start(s32[16]{0:T(128)} %copy-done.23) | copy-start | bytes 196
  182.0 8.6 %copy-start.22 = (f32[32]{0:T(128)S(1)}, f32[32]{0:T(128)}, u32[]{:S(2)}) copy-start(f32[32]{0:T(128)} %get-tuple-element.41) | copy-start | bytes 388
  182.0 26.1 %all-to-all-start = ((bf16[2,16,3,2048]{3,0,2,1:T(2,128)(2,1)}), bf16[2,16,3,2048]{3,0,2,1:T(2,128)(2,1)S(1)}, u32[]{:S(2)}, u32[]{:S(2)}) async-start(bf16[2,16,3,2048]{3,0,2,1:T(2,128)(2,1)} %copy.85), calls=%async_computation | async-start | bytes 786432 | tf_op jit(solution)/shard_map/all_to_all | solution.py:189
  187.0 64.1 %all-gather.5.cloned.1.call-start = ((), (), s32[]{:S(2)}) async-start(), calls=%async_computation.4 | async-start | bytes 4718592 | tf_op jit(solution)/shard_map/all_gather | solution.py:111
  187.6 109.9 %all-gather.7.cloned.1.call-start = ((), (), s32[]{:S(2)}) async-start(), calls=%async_computation.5 | async-start | bytes 4718592 | tf_op jit(solution)/shard_map/all_gather | solution.py:127
  187.8 8.5 %copy-start.10 = (bf16[2,32,4,128]{3,2,1,0:T(4,128)(2,1)}, bf16[2,32,4,128]{3,2,1,0:T(4,128)(2,1)S(1)}, u32[]{:S(2)}) copy-start(bf16[2,32,4,128]{3,2,1,0:T(4,128)(2,1)S(1)} %reshape.214) | copy-start | bytes 196612
  193.4 3.3 copy-start.6
  208.1 95.0 %all-to-all-start.2 = ((bf16[2,16,3,2048]{3,0,2,1:T(2,128)(2,1)}), bf16[2,16,3,2048]{3,0,2,1:T(2,128)(2,1)S(1)}, u32[]{:S(2)}, u32[]{:S(2)}) async-start(bf16[2,16,3,2048]{3,0,2,1:T(2,128)(2,1)} %copy.94), calls=%async_computation.2 | async-start | bytes 786432 | tf_op jit(solution)/shard_map/all_to_all | solution.py:189
  297.5 3.8 %copy-start.1 = (bf16[2,384,2048]{2,1,0:T(8,128)(2,1)S(1)}, bf16[2,384,2048]{2,1,0:T(8,128)(2,1)}, u32[]{:S(2)}) copy-start(bf16[2,384,2048]{2,1,0:T(8,128)(2,1)} %constant_dynamic-update-slice_fusion.2) | copy-start | bytes 9437188
  303.0 17.8 %all-to-all-start.1 = ((bf16[2,16,3,2048]{3,0,2,1:T(2,128)(2,1)}), bf16[2,16,3,2048]{3,0,2,1:T(2,128)(2,1)S(1)}, u32[]{:S(2)}, u32[]{:S(2)}) async-start(bf16[2,16,3,2048]{3,0,2,1:T(2,128)(2,1)} %bitcast.15), calls=%async_computation.1 | async-start | bytes 786432 | tf_op jit(solution)/shard_map/all_to_all | solution.py:199
  308.7 3.8 %copy-start.2 = (bf16[2,384,2048]{2,1,0:T(8,128)(2,1)S(1)}, bf16[2,384,2048]{2,1,0:T(8,128)(2,1)}, u32[]{:S(2)}) copy-start(bf16[2,384,2048]{2,1,0:T(8,128)(2,1)} %constant_dynamic-update-slice_fusion.2) | copy-start | bytes 9437188
  320.8 16.4 %copy-start.13 = (s32[256]{0:T(256)S(1)}, s32[256]{0:T(256)}, u32[]{:S(2)}) copy-start(s32[256]{0:T(256)} %copy-done.12) | copy-start | bytes 3076
  320.8 16.5 %copy-start.21 = (pred[256]{0:T(512)(128)(4,1)S(1)}, pred[256]{0:T(512)(128)(4,1)}, u32[]{:S(2)}) copy-start(pred[256]{0:T(512)(128)(4,1)} %copy-done.20) | copy-start | bytes 772
  320.8 15.8 %all-to-all-start.3 = ((bf16[2,16,3,2048]{3,0,2,1:T(2,128)(2,1)}), bf16[2,16,3,2048]{3,0,2,1:T(2,128)(2,1)S(1)}, u32[]{:S(2)}, u32[]{:S(2)}) async-start(bf16[2,16,3,2048]{3,0,2,1:T(2,128)(2,1)} %bitcast.30), calls=%async_computation.3 | async-start | bytes 786432 | tf_op jit(solution)/shard_map/all_to_all | solution.py:199
Sparse Core Ops, SparseCore 0:
  21.7 153.6 all-reduce.2
Sparse Core Ops, SparseCore 1:
  23.6 29.7 all-gather.8
  177.7 27.2 all-gather.10
  206.3 44.7 all-gather.4
  252.7 44.7 all-gather.6
where the time goes:
time: 348 us; the launch traced here: 347 us
  waiting for transfers between devices  249 us (72%)
  other arithmetic  20.8 us (6%)
  starting transfers between devices  20.5 us (6%)
  between operations  20.2 us (6%)
  local copies, waits for them, and re-layouts  18.5 us (5%)
  matrix products  17.3 us (5%)
    psum x1, waiting for transfers between devices, spread(): return lax.psum(jnp.where(mine, shard, jnp.zeros_like(shard)), axis)  148 us
    all_gather x1, waiting for transfers between devices, body(): lax.all_gather(replica_pair, 'dp', axis=1, tiled=True)  46.4 us
    all_gather x1, waiting for transfers between devices, body(): lax.all_gather(own_pair, 'dp', axis=1, tiled=True)  37 us
    all_to_all x2, waiting for transfers between devices, body(): lax.all_to_all(expert_out, 'ep', split_axis=1, concat_axis=1, tiled=True)  16.7 us
    all_to_all x2, starting transfers between devices, body(): lax.all_to_all(outgoing, 'ep', split_axis=1, concat_axis=1, tiled=True)  11 us
    all_to_all x2, starting transfers between devices, body(): lax.all_to_all(expert_out, 'ep', split_axis=1, concat_axis=1, tiled=True)  9.3 us
    dot_general x2, matrix products, body(): jnp.einsum('snd,skdf->sknf', slot_rows, slot_pair, preferred_element_type...  7.23 us
  transfers between devices with their start and end apart: 9, of which 5 were waited for; matrix products, arithmetic and copies ran while one was open for 12% of the time, Pallas kernels for 0%

commit v1 on v0

--- a/solution.py
+++ b/solution.py
@@ -11,6 +11,18 @@
 CAP = 3
 SLOTS = 2
 norm_epsilon = 1e-06
+
+
+def collect(array, axis, dim):
+    ways, here = (lax.axis_size(axis), lax.axis_index(axis))
+    grown, reach = (array, 1)
+    while reach < ways:
+        theirs = lax.ppermute(grown, axis, [(d, d ^ reach) for d in range(ways)])
+        mine_first = jnp.concatenate([grown, theirs], axis=dim)
+        theirs_first = jnp.concatenate([theirs, grown], axis=dim)
+        grown = jnp.where(here & reach == 0, mine_first, theirs_first)
+        reach = 2 * reach
+    return grown
 
 
 def spread(shard, axis, root):
@@ -108,7 +120,7 @@
     my_hot = jnp.sum(jnp.where(device_ids == my_device, replica_hot, 0))
     own_pair = jnp.concatenate([w_gate, w_up], axis=0)
     own_full_pair, own_full_down = (
-        lax.all_gather(own_pair, "dp", axis=1, tiled=True),
+        collect(own_pair, "dp", 1),
         lax.all_gather(w_down, "dp", axis=2, tiled=True),
     )
     replica_pair = jnp.zeros_like(own_pair)

time: 348 us -> 309 us (0.89)
  waiting for transfers between devices: 249 us -> 187 us
  matrix products: 17.3 us -> 25.1 us
  other arithmetic: 20.8 us -> 27.6 us
  local copies, waits for them, and re-layouts: 18.5 us -> 24.1 us
    all_gather x1 -> x0, waiting for transfers between devices: 37 us -> none  [body(): lax.all_gather(own_pair, 'dp', axis=1, tiled=True)]
    psum x1, waiting for transfers between devices: 148 us -> 133 us  [spread(): return lax.psum(jnp.where(mine, shard, jnp.zeros_like(shard)), axis)]
    all_gather x1, waiting for transfers between devices: 46.4 us -> 36.4 us  [body(): lax.all_gather(replica_pair, 'dp', axis=1, tiled=True)]
    dot_general x2, matrix products: 1.59 us -> 5.58 us  [attend(): jnp.einsum('rkgh,rckh->rkgc', grouped, keys_cached, preferred_element_typ...]
    select_n x0 -> x1, other arithmetic: none -> 3.9 us  [collect(): grown = jnp.where(here & reach == 0, mine_first, theirs_first)]
    unnamed x67 -> x111, local copies, waits for them, and re-layouts: 5.35 us -> 7.85 us
  transfers between devices with their start and end apart: 9 -> 9, of which waited for: 5 -> 4; matrix products, arithmetic and copies ran while one was open for 12% -> 20% of each run, Pallas kernels for 0% -> 0%
where the time goes in v1:
time: 309 us; the launch traced here: 308 us
  waiting for transfers between devices  187 us (61%)
  other arithmetic  27.6 us (9%)
  matrix products  25.1 us (8%)
  local copies, waits for them, and re-layouts  24.1 us (8%)
  starting transfers between devices  23.5 us (8%)
  between operations  20.2 us (7%)
    psum x1, waiting for transfers between devices, spread(): return lax.psum(jnp.where(mine, shard, jnp.zeros_like(shard)), axis)  133 us
    all_gather x1, waiting for transfers between devices, body(): lax.all_gather(replica_pair, 'dp', axis=1, tiled=True)  36.4 us
    all_to_all x2, waiting for transfers between devices, body(): lax.all_to_all(expert_out, 'ep', split_axis=1, concat_axis=1, tiled=True)  16.6 us
    all_to_all x2, starting transfers between devices, body(): lax.all_to_all(outgoing, 'ep', split_axis=1, concat_axis=1, tiled=True)  10.9 us
    all_to_all x2, starting transfers between devices, body(): lax.all_to_all(expert_out, 'ep', split_axis=1, concat_axis=1, tiled=True)  9.3 us
    unnamed x111, local copies, waits for them, and re-layouts  7.85 us
    dot_general x2, matrix products, body(): jnp.einsum('snd,skdf->sknf', slot_rows, slot_pair, preferred_element_type...  7.42 us
  transfers between devices with their start and end apart: 9, of which 4 were waited for; matrix products, arithmetic and copies ran while one was open for 20% of the time, Pallas kernels for 0%

profile of v1, /device:TPU:0, one launch (start us, length us, event | category | flops | bytes accessed | tf_op | source)
XLA Modules:
  0.0 307.6 jit_solution(3580631024851828832)
XLA Ops:
  8.1 1.5 fusion.144
  9.5 0.8 select_reduce_fusion.4
  10.3 2.7 fusion.145
  14.9 1.2 constant_dynamic-update-slice_fusion.1
  16.1 1.3 constant_dynamic-update-slice_fusion
  17.4 2.3 broadcast_select_fusion
  19.7 1.5 broadcast_select_fusion.3
  21.2 3.0 collective-permute-start
  26.3 0.6 reduce-window.14
  27.4 0.6 add_rsqrt_fusion
  28.0 1.3 convolution_convert_fusion.3
  29.4 1.5 reshape.259
  30.9 1.2 copy.85
  32.1 6.0 %all-to-all-start = ((bf16[2,16,3,2048]{3,0,2,1:T(2,128)(2,1)}), bf16[2,16,3,2048]{3,0,2,1:T(2,128)(2,1)}, u32[]{:S(2)}, u32[]{:S(2)}) async-start(bf16[2,16,3,2048]{3,0,2,1:T(2,128)(2,1)} %copy.85), calls=%async_computation | async-start | bytes 786432 | tf_op jit(solution)/shard_map/all_to_all | solution.py:201
  38.2 0.5 all-gather.6.cloned.1.call-update
  38.7 1.1 slice_bitcast_fusion.1
  40.6 1.3 fusion.139
  41.9 0.7 copy.117
  42.6 0.6 reshape.269
  43.3 0.8 copy.118
  45.9 0.3 fusion.14
  46.5 0.6 copy-done.34
  47.0 0.6 reduce-window.16
  47.9 1.3 select_reduce_fusion.3
  49.2 133.4 %all-reduce.3.cloned.1.call-done = (bf16[1,384,1024]{2,1,0:T(8,128)(2,1)}, bf16[1,384,1024]{2,1,0:T(8,128)(2,1)}, bf16[1,384,1024]{2,1,0:T(8,128)(2,1)}, bf16[2,...) async-done(((bf16[1,384,1024]{2,1,0:T(8,128)(2,1)}, bf16[1,384,1024]{2,1,0:T(8,128)(2,1)}, bf16[1,384,1024]{2,1,0:T(8,128)(2,1)}, ...) | async-done | bytes 7077904 | tf_op jit(solution)/shard_map/psum | solution.py:30
  182.6 2.1 select_select_fusion.1
  185.1 2.1 select_reduce_fusion.1
  187.3 1.4 select_reduce_fusion.2
  188.8 3.5 %fusion.23 = (f32[32,4,8]{2,1,0:T(4,128)}, f32[32,4,8]{2,1,0:T(4,128)S(1)}, f32[32,4,8,32]{3,2,1,0:T(8,128)}) fusion(f32[32,4,8,32]{3,2,1,0:T(8,128)S(1)} %get-tuple-element.35, f32[32,4,8]{2,1,0:T(4,128)S(1)} %max.14, pred[32,32]{1,0:T(8,128)(4,1)S(1)} %iota_compare_fusion.23, bf16[32,4,8,128]{3,2,1,0:T(8,128)(2,1)} %bitcast.165, ...), kind=kOutput, calls=%fused_computation.57 | convolution fusion | flops 8583168 | bytes 1586176 | tf_op jit(solution)/shard_map/rkgh,rckh->rkgc/dot_general | solution.py:56
  192.5 1.4 select_select_fusion
  194.1 1.1 slice_reduce_fusion.3
  195.1 1.4 convolution_convert_fusion.1
  196.5 1.1 fusion.168
  197.7 0.6 reshape.271
  198.6 1.4 reshape.264
  200.1 1.2 copy.94
  201.3 0.9 add.119
  202.3 1.4 fusion.24
  203.7 0.9 add.121
  204.6 1.3 fusion.78
  206.0 0.4 fusion.79
  206.4 0.5 fusion.6
  207.0 0.5 fusion.7
  207.5 2.7 constant_dynamic-update-slice_fusion.3
  210.3 3.9 %maximum_select_fusion = bf16[1,2,2048,384]{3,2,1,0:T(8,128)(2,1)} fusion(bf16[1,2,1024,384]{3,2,1,0:T(8,128)(2,1)} %bitcast.8, bf16[1,2,1024,384]{3,2,1,0:T(8,128)(2,1)S(1)} %bitcast.160, pred[]{:T(512)S(6)} %eq.293), kind=kLoop, calls=%fused_computation.3 | loop fusion | flops 14155776 | bytes 6291457 | tf_op jit(solution)/shard_map/jit(_where)/select_n | solution.py:23
  214.2 2.8 constant_dynamic-update-slice_fusion.2
  217.0 4.9 %all-to-all-start.2 = ((bf16[2,16,3,2048]{3,0,2,1:T(2,128)(2,1)}), bf16[2,16,3,2048]{3,0,2,1:T(2,128)(2,1)S(1)}, u32[]{:S(2)}, u32[]{:S(2)}) async-start(bf16[2,16,3,2048]{3,0,2,1:T(2,128)(2,1)} %copy.94), calls=%async_computation.2 | async-start | bytes 786432 | tf_op jit(solution)/shard_map/all_to_all | solution.py:201
  221.9 36.4 %all-gather.4.cloned.1.call-done = bf16[2,2048,384]{2,1,0:T(8,128)(2,1)} async-done(((bf16[2,1024,384]{2,1,0:T(8,128)(2,1)}), bf16[2,2048,384]{2,1,0:T(8,128)(2,1)}) %all-gather.4.cloned.1.call-update) | async-done | bytes 3145744 | tf_op jit(solution)/shard_map/all_gather | solution.py:139
  258.3 3.8 %convolution_bitcast_fusion = f32[2,2,48,384]{3,2,1,0:T(8,128)S(1)} fusion(bf16[2,48,2048,1]{2,0,1,3:T(2,128)(2,1)} %bitcast.12, bf16[1,2,2048,384]{3,2,1,0:T(8,128)(2,1)} %bitcast.174, bf16[1,2,2048,384]{3,2,1,0:T(8,128)(2,1)} %maximum_select_fusion), kind=kOutput, calls=%fused_computation.25 | convolution fusion | flops 314572800 | bytes 6979584 | tf_op jit(solution)/shard_map/snd,skdf->sknf/dot_general | solution.py:203
  262.1 0.7 convolution_convert_fusion.2
  262.8 1.2 copy.88
  264.0 5.6 %all-to-all-start.1 = ((bf16[2,16,3,2048]{3,0,2,1:T(2,128)(2,1)}), bf16[2,16,3,2048]{3,0,2,1:T(2,128)(2,1)S(1)}, u32[]{:S(2)}, u32[]{:S(2)}) async-start(bf16[2,16,3,2048]{3,0,2,1:T(2,128)(2,1)} %bitcast.16), calls=%async_computation.1 | async-start | bytes 786432 | tf_op jit(solution)/shard_map/all_to_all | solution.py:211
  269.6 3.6 %fusion.8 = f32[2,2,48,384]{3,2,0,1:T(8,128)S(1)} fusion(bf16[2,48,2048]{2,0,1:T(2,128)(2,1)S(1)} %bitcast.163, bf16[1,2,2048,384]{3,2,1,0:T(8,128)(2,1)} %bitcast.175, bf16[1,2,2048,384]{3,2,1,0:T(8,128)(2,1)} %maximum_select_fusion), kind=kOutput, calls=%fused_computation.24 | convolution fusion | flops 305135616 | bytes 6979584 | tf_op jit(solution)/shard_map/snd,skdf->sknf/dot_general | solution.py:203
  273.4 0.6 convolution_convert_fusion
  274.0 1.2 copy.97
  275.2 6.6 %all-to-all-done.1 = bf16[2,16,3,2048]{3,0,2,1:T(2,128)(2,1)S(1)} async-done(((bf16[2,16,3,2048]{3,0,2,1:T(2,128)(2,1)}), bf16[2,16,3,2048]{3,0,2,1:T(2,128)(2,1)S(1)}, u32[]{:S(2)}, u32[]{:S(2)}) %all-to-all-start.1) | async-done | bytes 393248 | tf_op jit(solution)/shard_map/all_to_all | solution.py:211
  281.8 3.7 %all-to-all-start.3 = ((bf16[2,16,3,2048]{3,0,2,1:T(2,128)(2,1)}), bf16[2,16,3,2048]{3,0,2,1:T(2,128)(2,1)S(1)}, u32[]{:S(2)}, u32[]{:S(2)}) async-start(bf16[2,16,3,2048]{3,0,2,1:T(2,128)(2,1)} %bitcast.31), calls=%async_computation.3 | async-start | bytes 786432 | tf_op jit(solution)/shard_map/all_to_all | solution.py:211
  286.1 0.8 pad_maximum_fusion.1
  287.2 0.3 reshape.262
  287.6 10.0 %all-to-all-done.3 = bf16[2,16,3,2048]{3,0,2,1:T(2,128)(2,1)S(1)} async-done(((bf16[2,16,3,2048]{3,0,2,1:T(2,128)(2,1)}), bf16[2,16,3,2048]{3,0,2,1:T(2,128)(2,1)S(1)}, u32[]{:S(2)}, u32[]{:S(2)}) %all-to-all-start.3) | async-done | bytes 393248 | tf_op jit(solution)/shard_map/all_to_all | solution.py:211
  297.9 0.3 reshape.267
  298.2 0.5 fusion.5
  298.8 0.5 fusion.4
  299.3 0.7 pad_maximum_fusion.2
  (177 shorter events, 6.2 us)
Async XLA Ops:
  8.0 198.4 %copy-start = (bf16[32,32,512]{2,1,0:T(8,128)(2,1)S(1)}, bf16[32,32,512]{2,1,0:T(8,128)(2,1)}, u32[]{:S(2)}) copy-start(bf16[32,32,512]{2,1,0:T(8,128)(2,1)} %param.30) | copy-start | bytes 3145732
  8.0 174.6 %all-reduce.3.cloned.1.call-start = ((), (), s32[]{:S(2)}) async-start(), calls=%async_computation.7 | async-start | bytes 14155776 | tf_op jit(solution)/shard_map/psum | solution.py:30
  17.4 2.3 copy-start.3
  21.2 3.1 %copy-start.27 = (s32[2,32,8]{1,2,0:T(8,128)S(1)}, s32[2,32,8]{1,2,0:T(8,128)}, u32[]{:S(2)}) copy-start(s32[2,32,8]{1,2,0:T(8,128)} %param.20) | copy-start | bytes 6148
  21.2 3.3 %copy-start.28 = (s32[2,32,8]{1,2,0:T(8,128)S(1)}, s32[2,32,8]{1,2,0:T(8,128)}, u32[]{:S(2)}) copy-start(s32[2,32,8]{1,2,0:T(8,128)} %param.21) | copy-start | bytes 6148
  21.2 3.5 %copy-start.45 = (s32[3]{0:T(128)S(1)}, s32[3]{0:T(128)}, u32[]{:S(2)}) copy-start(s32[3]{0:T(128)} %param.23) | copy-start | bytes 40
  21.2 3.5 %copy-start.50 = (s32[16]{0:T(128)S(1)}, s32[16]{0:T(128)}, u32[]{:S(2)}) copy-start(s32[16]{0:T(128)} %param.24) | copy-start | bytes 196
  21.2 5.9 %copy-start.31 = (bf16[2048]{0:T(1024)(128)(2,1)S(1)}, bf16[2048]{0:T(1024)(128)(2,1)}, u32[]{:S(2)}) copy-start(bf16[2048]{0:T(1024)(128)(2,1)} %param.18) | copy-start | bytes 12292
  21.2 6.0 %copy-start.4 = (bf16[2,32,2048]{2,1,0:T(8,128)(2,1)S(1)}, bf16[2,32,2048]{2,1,0:T(8,128)(2,1)}, u32[]{:S(2)}) copy-start(bf16[2,32,2048]{2,1,0:T(8,128)(2,1)} %param.17) | copy-start | bytes 786436
  21.2 189.0 %collective-permute-start = (bf16[2,1024,384]{2,1,0:T(8,128)(2,1)S(1)}, bf16[2,1024,384]{2,1,0:T(8,128)(2,1)}, u32[]{:S(2)}, u32[]{:S(2)}) collective-permute-start(bf16[2,1024,384]{2,1,0:T(8,128)(2,1)S(1)} %constant_dynamic-update-slice_fusion), channel_id=1, source_target_pairs={{0,1},{1,0},{2,3},{3,2},{4,5},{5,4},{6,7},{7,6},{8,9},{9,8},{10,11... | collective-permute-start | bytes 4718600 | tf_op jit(solution)/shard_map/ppermute | solution.py:20
  24.7 0.9 copy-start.43
  25.0 0.5 copy-start.51
  25.5 17.1 %copy-start.15 = (bf16[2,32,512]{2,1,0:T(8,128)(2,1)S(1)}, bf16[2,32,512]{2,1,0:T(8,128)(2,1)}, u32[]{:S(2)}) copy-start(bf16[2,32,512]{2,1,0:T(8,128)(2,1)} %param.31) | copy-start | bytes 196612
  27.4 16.7 %copy-start.37 = (pred[256]{0:T(512)(128)(4,1)}, pred[256]{0:T(512)(128)(4,1)S(1)}, u32[]{:S(2)}) copy-start(pred[256]{0:T(512)(128)(4,1)S(1)} %add_compare_fusion.1) | copy-start | bytes 772
  28.0 16.1 %copy-start.19 = (s32[256]{0:T(256)}, s32[256]{0:T(256)S(1)}, u32[]{:S(2)}) copy-start(s32[256]{0:T(256)S(1)} %add_add_fusion.1) | copy-start | bytes 3076
  28.0 12.0 %copy-start.52 = (s32[16]{0:T(128)S(1)}, s32[16]{0:T(128)}, u32[]{:S(2)}) copy-start(s32[16]{0:T(128)} %copy-done.51) | copy-start | bytes 196
  28.0 17.9 %copy-start.44 = (s32[16]{0:T(128)S(1)}, s32[16]{0:T(128)}, u32[]{:S(2)}) copy-start(s32[16]{0:T(128)} %copy-done.43) | copy-start | bytes 196
  32.1 184.9 %all-to-all-start = ((bf16[2,16,3,2048]{3,0,2,1:T(2,128)(2,1)}), bf16[2,16,3,2048]{3,0,2,1:T(2,128)(2,1)}, u32[]{:S(2)}, u32[]{:S(2)}) async-start(bf16[2,16,3,2048]{3,0,2,1:T(2,128)(2,1)} %copy.85), calls=%async_computation | async-start | bytes 786432 | tf_op jit(solution)/shard_map/all_to_all | solution.py:201
  38.1 169.4 %all-gather.6.cloned.1.call-start = ((), (), s32[]{:S(2)}) async-start(), calls=%async_computation.5 | async-start | bytes 2359296 | tf_op jit(solution)/shard_map/all_gather | solution.py:124
  38.7 175.5 %all-gather.8.cloned.1.call-start = ((), (), s32[]{:S(2)}) async-start(), calls=%async_computation.6 | async-start | bytes 2359296 | tf_op jit(solution)/shard_map/all_gather | solution.py:140
  40.6 144.2 %copy-start.23 = (s32[256]{0:T(256)}, s32[256]{0:T(256)S(1)}, u32[]{:S(2)}) copy-start(s32[256]{0:T(256)S(1)} %and_select_fusion) | copy-start | bytes 3076
  41.9 143.1 %copy-start.42 = (s32[32]{0:T(128)S(1)}, s32[32]{0:T(128)}, u32[]{:S(2)}) copy-start(s32[32]{0:T(128)} %param.33) | copy-start | bytes 388
  42.6 142.5 %copy-start.8 = (bf16[4,8,32,128]{3,2,1,0:T(8,128)(2,1)S(1)}, bf16[4,8,32,128]{3,2,1,0:T(8,128)(2,1)}, u32[]{:S(2)}) copy-start(bf16[4,8,32,128]{3,2,1,0:T(8,128)(2,1)} %copy.117) | copy-start | bytes 786436
  46.2 1.4 copy-start.32
  46.4 0.6 copy-start.34
  46.5 138.3 %copy-start.25 = (s32[256]{0:T(256)}, s32[256]{0:T(256)S(1)}, u32[]{:S(2)}) copy-start(s32[256]{0:T(256)S(1)} %convert_add_fusion) | copy-start | bytes 3076
  47.8 139.4 %copy-start.30 = (s32[32,3]{0,1:T(4,128)}, s32[32,3]{0,1:T(4,128)S(1)}, u32[]{:S(2)}) copy-start(s32[32,3]{0,1:T(4,128)S(1)} %reduce-window.19) | copy-start | bytes 1156
  47.9 139.4 %copy-start.46 = (pred[2]{0:T(512)(128)(4,1)}, pred[2]{0:T(512)(128)(4,1)S(1)}, u32[]{:S(2)}) copy-start(pred[2]{0:T(512)(128)(4,1)S(1)} %iota_compare_fusion.28) | copy-start | bytes 10
  49.2 147.3 %copy-start.12 = (f32[32,4,8,2]{2,3,1,0:T(2,128)}, f32[32,4,8,2]{2,3,1,0:T(2,128)S(1)}, u32[]{:S(2)}) copy-start(f32[32,4,8,2]{2,3,1,0:T(2,128)S(1)} %get-tuple-element.37) | copy-start | bytes 24580
  184.8 73.5 %all-gather.4.cloned.1.call-start = ((), (), s32[]{:S(2)}) async-start(), calls=%async_computation.4 | async-start | bytes 4718592 | tf_op jit(solution)/shard_map/all_gather | solution.py:139
  185.0 7.3 %copy-start.26 = (s32[256]{0:T(256)S(1)}, s32[256]{0:T(256)}, u32[]{:S(2)}) copy-start(s32[256]{0:T(256)} %copy-done.25) | copy-start | bytes 3076
  185.0 7.4 %copy-start.5 = (bf16[2,1024,384]{2,1,0:T(8,128)(2,1)S(1)}, bf16[2,1024,384]{2,1,0:T(8,128)(2,1)}, u32[]{:S(2)}) copy-start(bf16[2,1024,384]{2,1,0:T(8,128)(2,1)} %get-tuple-element.17) | copy-start | bytes 4718596
  185.0 7.4 %copy-start.6 = (bf16[2,1024,384]{2,1,0:T(8,128)(2,1)S(1)}, bf16[2,1024,384]{2,1,0:T(8,128)(2,1)}, u32[]{:S(2)}) copy-start(bf16[2,1024,384]{2,1,0:T(8,128)(2,1)} %get-tuple-element.18) | copy-start | bytes 4718596
  185.0 7.4 %copy-start.7 = (bf16[2,1024,384]{2,1,0:T(8,128)(2,1)S(1)}, bf16[2,1024,384]{2,1,0:T(8,128)(2,1)}, u32[]{:S(2)}) copy-start(bf16[2,1024,384]{2,1,0:T(8,128)(2,1)} %get-tuple-element.19) | copy-start | bytes 4718596
  187.3 5.0 %copy-start.10 = (f32[32,4,8,32]{3,2,1,0:T(8,128)}, f32[32,4,8,32]{3,2,1,0:T(8,128)S(1)}, u32[]{:S(2)}) copy-start(f32[32,4,8,32]{3,2,1,0:T(8,128)S(1)} %get-tuple-element.35) | copy-start | bytes 393220
  187.3 5.0 %slice-start = ((s32[32,3]{0,1:T(4,128)}), s32[32,2]{0,1:T(2,128)S(1)}, s32[]{:S(2)}) async-start(s32[32,3]{0,1:T(4,128)} %copy-done.30), calls=%async_computation.8 | async-start | bytes 2048 | tf_op jit(solution)/shard_map/slice.3
  187.3 9.2 %copy-start.48 = (pred[2]{0:T(512)(128)(4,1)}, pred[2]{0:T(512)(128)(4,1)S(1)}, u32[]{:S(2)}) copy-start(pred[2]{0:T(512)(128)(4,1)S(1)} %iota_compare_fusion.27) | copy-start | bytes 10
  188.8 7.7 %copy-start.13 = (f32[32,4,8,2]{2,3,1,0:T(2,128)}, f32[32,4,8,2]{2,3,1,0:T(2,128)S(1)}, u32[]{:S(2)}) copy-start(f32[32,4,8,2]{2,3,1,0:T(2,128)S(1)} %get-tuple-element.40) | copy-start | bytes 24580
  192.4 1.6 copy-start.24
  192.4 1.6 copy-start.33
  192.4 1.6 copy-start.35
  192.5 1.6 copy-start.29
  192.5 2.7 copy-start.41
  192.5 4.0 %copy-start.47 = (pred[2]{0:T(512)(128)(4,1)S(1)}, pred[2]{0:T(512)(128)(4,1)}, u32[]{:S(2)}) copy-start(pred[2]{0:T(512)(128)(4,1)} %copy-done.46) | copy-start | bytes 10
  192.5 5.2 %copy-start.16 = (bf16[2,32,512]{2,1,0:T(8,128)(2,1)S(1)}, bf16[2,32,512]{2,1,0:T(8,128)(2,1)}, u32[]{:S(2)}) copy-start(bf16[2,32,512]{2,1,0:T(8,128)(2,1)} %param.32) | copy-start | bytes 196612
  194.0 4.3 %copy-start.39 = (pred[256]{0:T(512)(128)(4,1)}, pred[256]{0:T(512)(128)(4,1)S(1)}, u32[]{:S(2)}) copy-start(pred[256]{0:T(512)(128)(4,1)S(1)} %add_compare_fusion) | copy-start | bytes 772
  194.1 4.5 %copy-start.21 = (s32[256]{0:T(256)}, s32[256]{0:T(256)S(1)}, u32[]{:S(2)}) copy-start(s32[256]{0:T(256)S(1)} %add_add_fusion) | copy-start | bytes 3076
  200.1 5.9 %copy-start.14 = (f32[32,4,8,2]{2,3,1,0:T(2,128)S(1)}, f32[32,4,8,2]{2,3,1,0:T(2,128)}, u32[]{:S(2)}) copy-start(f32[32,4,8,2]{2,3,1,0:T(2,128)} %copy-done.13) | copy-start | bytes 24580
  200.1 5.9 %copy-start.17 = (bf16[2,32,4,128]{3,2,1,0:T(4,128)(2,1)S(1)}, bf16[2,32,4,128]{3,2,1,0:T(4,128)(2,1)}, u32[]{:S(2)}) copy-start(bf16[2,32,4,128]{3,2,1,0:T(4,128)(2,1)} %reshape.271) | copy-start | bytes 196612
  200.1 5.9 %copy-start.49 = (pred[2]{0:T(512)(128)(4,1)S(1)}, pred[2]{0:T(512)(128)(4,1)}, u32[]{:S(2)}) copy-start(pred[2]{0:T(512)(128)(4,1)} %copy-done.48) | copy-start | bytes 10
  201.3 5.1 %copy-start.11 = (f32[32,4,8,32]{3,2,1,0:T(8,128)S(1)}, f32[32,4,8,32]{3,2,1,0:T(8,128)}, u32[]{:S(2)}) copy-start(f32[32,4,8,32]{3,2,1,0:T(8,128)} %copy-done.10) | copy-start | bytes 393220
  206.0 1.0 copy-start.9
  217.0 47.0 %all-to-all-start.2 = ((bf16[2,16,3,2048]{3,0,2,1:T(2,128)(2,1)}), bf16[2,16,3,2048]{3,0,2,1:T(2,128)(2,1)S(1)}, u32[]{:S(2)}, u32[]{:S(2)}) async-start(bf16[2,16,3,2048]{3,0,2,1:T(2,128)(2,1)} %copy.94), calls=%async_computation.2 | async-start | bytes 786432 | tf_op jit(solution)/shard_map/all_to_all | solution.py:201
  258.3 3.9 %copy-start.1 = (bf16[2,384,2048]{2,1,0:T(8,128)(2,1)S(1)}, bf16[2,384,2048]{2,1,0:T(8,128)(2,1)}, u32[]{:S(2)}) copy-start(bf16[2,384,2048]{2,1,0:T(8,128)(2,1)} %constant_dynamic-update-slice_fusion.2) | copy-start | bytes 9437188
  264.0 17.8 %all-to-all-start.1 = ((bf16[2,16,3,2048]{3,0,2,1:T(2,128)(2,1)}), bf16[2,16,3,2048]{3,0,2,1:T(2,128)(2,1)S(1)}, u32[]{:S(2)}, u32[]{:S(2)}) async-start(bf16[2,16,3,2048]{3,0,2,1:T(2,128)(2,1)} %bitcast.16), calls=%async_computation.1 | async-start | bytes 786432 | tf_op jit(solution)/shard_map/all_to_all | solution.py:211
  269.6 3.8 %copy-start.2 = (bf16[2,384,2048]{2,1,0:T(8,128)(2,1)S(1)}, bf16[2,384,2048]{2,1,0:T(8,128)(2,1)}, u32[]{:S(2)}) copy-start(bf16[2,384,2048]{2,1,0:T(8,128)(2,1)} %constant_dynamic-update-slice_fusion.2) | copy-start | bytes 9437188
  273.4 12.4 %copy-start.36 = (f32[32]{0:T(128)S(1)}, f32[32]{0:T(128)}, u32[]{:S(2)}) copy-start(f32[32]{0:T(128)} %get-tuple-element.5) | copy-start | bytes 388
  273.4 12.5 %copy-start.18 = (f32[1,32,8]{1,2,0:T(8,128)S(1)}, f32[1,32,8]{1,2,0:T(8,128)}, u32[]{:S(2)}) copy-start(f32[1,32,8]{1,2,0:T(8,128)} %get-tuple-element.33) | copy-start | bytes 3076
  281.8 16.4 %copy-start.20 = (s32[256]{0:T(256)S(1)}, s32[256]{0:T(256)}, u32[]{:S(2)}) copy-start(s32[256]{0:T(256)} %copy-done.19) | copy-start | bytes 3076
  281.8 16.5 %copy-start.38 = (pred[256]{0:T(512)(128)(4,1)S(1)}, pred[256]{0:T(512)(128)(4,1)}, u32[]{:S(2)}) copy-start(pred[256]{0:T(512)(128)(4,1)} %copy-done.37) | copy-start | bytes 772
  281.8 15.8 %all-to-all-start.3 = ((bf16[2,16,3,2048]{3,0,2,1:T(2,128)(2,1)}), bf16[2,16,3,2048]{3,0,2,1:T(2,128)(2,1)S(1)}, u32[]{:S(2)}, u32[]{:S(2)}) async-start(bf16[2,16,3,2048]{3,0,2,1:T(2,128)(2,1)} %bitcast.31), calls=%async_computation.3 | async-start | bytes 786432 | tf_op jit(solution)/shard_map/all_to_all | solution.py:211
  285.5 13.3 %copy-start.22 = (s32[256]{0:T(256)S(1)}, s32[256]{0:T(256)}, u32[]{:S(2)}) copy-start(s32[256]{0:T(256)} %copy-done.21) | copy-start | bytes 3076
  285.5 13.3 %copy-start.40 = (pred[256]{0:T(512)(128)(4,1)S(1)}, pred[256]{0:T(512)(128)(4,1)}, u32[]{:S(2)}) copy-start(pred[256]{0:T(512)(128)(4,1)} %copy-done.39) | copy-start | bytes 772
Sparse Core Ops, SparseCore 0:
  21.3 161.2 all-reduce.2
Sparse Core Ops, SparseCore 1:
  40.1 35.5 all-gather.5
  184.8 27.2 all-gather.7
  213.5 44.7 all-gather.3
